TPU v7x, 32 devices: a whole 2x2x4 slice. The times are simulated.
32 devices in a mesh: tower: 2 (over core), batch: 16 (over z, y, x).
Axes of the slice: x: 2, y: 2, z: 4, core: 2. Of those that a mesh axis runs over, the one named last changes fastest.
Arguments:
- shard_ids: int32 [3, 1664, 10, 8], P(None, 'batch'), may hold values from 0 to 31, all different within a row; in each aligned block of 1040 rows (0 to 1039, 1040 to 2079, ..., all dimensions but the last counted through in order) at most 1040 rows name the same one
- local_rows: int32 [3, 1664, 10, 8], P(None, 'batch'), may hold values from 0 to 32767
- bag_counts: int32 [3, 1664, 39], P(None, 'batch'), may hold values from 1 to 24, 80 in all within a row
- click_labels: int32 [3, 1664], P(None, 'batch'), may hold values 0 or 1
- sample_weights: int32 [3, 1664], P(None, 'batch'), may hold values from 1 to 5
- embed_table: float32 [11, 1048576], P(None, ('tower', 'batch')), may hold values from -1 to 1
- table_first: float32 [11, 1048576], P(None, ('tower', 'batch')), may hold values from -1 to 1
- table_second: float32 [11, 1048576], P(None, ('tower', 'batch')), may hold values from 0 to 1
- dense_params: float32 [621632], P(('tower', 'batch')), may hold values from -1.5 to 1.5
- dense_first: float32 [621632], P(('tower', 'batch')), may hold values from -1 to 1
- dense_second: float32 [621632], P(('tower', 'batch')), may hold values from 0 to 1
Outputs:
- table_new: float32 [11, 1048576], P(None, ('tower', 'batch'))
- table_first_new: float32 [11, 1048576], P(None, ('tower', 'batch'))
- table_second_new: float32 [11, 1048576], P(None, ('tower', 'batch'))
- table_copy: bfloat16 [11, 1048576], P(None, ('tower', 'batch'))
- dense_new: float32 [621632], P(('tower', 'batch'))
- dense_first_new: float32 [621632], P(('tower', 'batch'))
- dense_second_new: float32 [621632], P(('tower', 'batch'))
- dense_copy: bfloat16 [621632], P(('tower', 'batch'))
- loss_value: float32 [], replicated
Inputs may be any that keep to these rules, and one draw needn't show every extreme that they name: `shard_ids`: within each group of 8 the shards differ; over the ids of one device's samples in one micro-batch (aligned blocks of 104 samples) no shard is named more than 1040 times, a bound that some block reaches. `bag_counts`: the 39 counts of each sample add up to 80.
All inputs are finite; a program needn't handle non-finite values. No bound on the sum of `click_labels` on one device may be relied on, other than what follows from the above.
Results may differ from a plain program's by a relative error of at most 0.004.
The roundings to bfloat16 on the way count: a program that leaves them out, or rounds other values in their place, can miss the bound.
Values may be sent and summed in bfloat16 or wider, within the bound.
A program may use at most 192 MiB of HBM per device.

v0:
```python
from functools import partial

import jax
import jax.numpy as jnp
from jax import lax
from jax.sharding import PartitionSpec as P

FIELDS = 39
EMB = 10
MAPS = 200
HID = 400
IDS_SAMP = 80


highest = lax.Precision.HIGHEST
beta_one = 0.9
beta_two = 0.999
epsilon = 1e-08
decay_rate = 0.15
rate_table = 0.1
rate_dense = 0.05
step_count = 10
block_width = 128


def adam_update(weight, first_old, second_old, gradient, step_rate):
    first_new = beta_one * first_old + (1.0 - beta_one) * gradient
    second_new = beta_two * second_old + (1.0 - beta_two) * gradient * gradient
    first_hat = first_new / (1.0 - beta_one**step_count)
    second_hat = second_new / (1.0 - beta_two**step_count)
    weight_new = weight - step_rate * (
        first_hat / (jnp.sqrt(second_hat) + epsilon) + decay_rate * weight
    )
    return (weight_new, first_new, second_new)


def field_table(counts_here):
    bag_ends = jnp.cumsum(counts_here, axis=-1)
    positions = jnp.arange(IDS_SAMP, dtype=jnp.int32)
    field_of = jnp.sum(
        (positions[None, :, None] >= bag_ends[:, None, :]).astype(jnp.int32), axis=-1
    )
    return (field_of[:, :, None] == jnp.arange(FIELDS, dtype=jnp.int32)[None, None, :]).astype(
        jnp.float32
    )


def cin_pairs(embedded):
    turned = jnp.swapaxes(embedded, 1, 2)
    pair_terms = turned[:, :, :, None] * turned[:, :, None, :]
    return pair_terms.reshape(turned.shape[0], EMB, FIELDS * FIELDS)


def unpack(flat_params):
    amounts = [MAPS * FIELDS * FIELDS, MAPS, FIELDS * EMB * HID, HID, HID * HID, HID, HID, 1]
    layouts = [
        (MAPS, FIELDS * FIELDS),
        (MAPS,),
        (FIELDS * EMB, HID),
        (HID,),
        (HID, HID),
        (HID,),
        (HID,),
        (1,),
    ]
    pieces = []
    offset = 0
    for amount, layout in zip(amounts, layouts):
        pieces.append(flat_params[offset : offset + amount].reshape(layout))
        offset += amount
    return tuple(pieces)


def pack(gradients, total_size):
    flat_grad = jnp.concatenate([piece.reshape(-1) for piece in gradients])
    return jnp.concatenate([flat_grad, jnp.zeros((total_size - flat_grad.shape[0],), jnp.float32)])


def place_ids(owner_ids, tower_at, batch_count, capacity):
    is_mine = owner_ids // batch_count == tower_at
    target = jnp.where(is_mine, owner_ids % batch_count, batch_count)
    id_count = target.shape[0]
    padding = -id_count % block_width
    one_hot = (target[:, None] == jnp.arange(batch_count + 1, dtype=jnp.int32)[None, :]).astype(
        jnp.float32
    )
    one_hot = jnp.concatenate([one_hot, jnp.zeros((padding, batch_count + 1), jnp.float32)], axis=0)
    grouped = one_hot.reshape(-1, block_width, batch_count + 1)
    lower = (jnp.arange(block_width)[:, None] > jnp.arange(block_width)[None, :]).astype(
        jnp.float32
    )
    inside = jnp.einsum("ij,njt->nit", lower, grouped, precision=highest)
    totals = jnp.sum(grouped, axis=1)
    before = jnp.cumsum(totals, axis=0) - totals
    rank = jnp.sum((inside + before[:, None, :]) * grouped, axis=-1).reshape(-1).astype(jnp.int32)
    tallies = jnp.sum(totals, axis=0).astype(jnp.int32)[:batch_count]
    slot_ids = jnp.where(is_mine, target * capacity + rank, batch_count * capacity)
    ordering = jnp.argsort(target, stable=True)
    starts = jnp.cumsum(tallies) - tallies
    within = jnp.arange(capacity, dtype=jnp.int32)[None, :]
    source = ordering[jnp.minimum(starts[:, None] + within, id_count - 1)]
    valid = within < tallies[:, None]
    return (slot_ids, source, valid)


def lookup(requests, table_low):
    wanted = lax.all_to_all(requests, "batch", split_axis=1, concat_axis=1, tiled=True)
    is_valid = wanted >= 0
    taken = jnp.moveaxis(jnp.take(table_low, jnp.maximum(wanted, 0), axis=1), 0, -1)
    found_rows = jnp.where(is_valid[..., None], taken, jnp.zeros((), jnp.bfloat16))
    answered = lax.all_to_all(found_rows, "batch", split_axis=1, concat_axis=1, tiled=True)
    return (answered, wanted)


def deliver(sendable):
    return lax.all_to_all(
        sendable.astype(jnp.bfloat16), "batch", split_axis=1, concat_axis=1, tiled=True
    ).astype(sendable.dtype)


def scatter_rows(delivered, served, rows_dev):
    places = jnp.where(served >= 0, served, rows_dev).reshape(-1)
    columns = delivered.shape[-1]
    flat_grads = jnp.swapaxes(delivered.reshape(-1, columns), 0, 1)
    return jnp.zeros((columns, rows_dev), jnp.float32).at[:, places].add(flat_grads, mode="drop")


def cin_forward(pooled, params):
    cin_w, cin_u = (params[0], params[1])
    samples = pooled.shape[0]
    pair_terms = cin_pairs(pooled[:, :, :EMB]).astype(jnp.bfloat16)
    map_values = lax.dot_general(
        pair_terms, cin_w, (((2,), (1,)), ((), ())), preferred_element_type=jnp.float32
    )
    map_sum = jnp.sum(map_values, axis=1)
    logits = jnp.dot(map_sum, cin_u.astype(jnp.float32), precision=highest)
    spare = jnp.zeros((samples, HID), jnp.float32)
    return (logits, (map_sum, spare, spare))


def deep_forward(pooled, params):
    cin_w, cin_u, w_one, b_one, w_two, b_two, w_three, bias = params
    samples = pooled.shape[0]
    flat_embed = pooled[:, :, :EMB].reshape(samples, FIELDS * EMB).astype(jnp.bfloat16)
    pre_one = jnp.dot(flat_embed, w_one, preferred_element_type=jnp.float32) + b_one.astype(
        jnp.float32
    )
    hidden_one = jax.nn.relu(pre_one).astype(jnp.bfloat16)
    pre_two = jnp.dot(hidden_one, w_two, preferred_element_type=jnp.float32) + b_two.astype(
        jnp.float32
    )
    deep_logits = jnp.dot(jax.nn.relu(pre_two), w_three.astype(jnp.float32), precision=highest)
    logits = deep_logits + jnp.sum(pooled[:, :, EMB], axis=1) + bias.astype(jnp.float32)[0]
    return (logits, (jnp.zeros((samples, cin_u.shape[0]), jnp.float32), pre_one, pre_two))


def cin_backward(pooled, grad_logits, stored, params, total_size):
    cin_w, cin_u = (params[0], params[1])
    embedded = pooled[:, :, :EMB]
    samples = embedded.shape[0]
    pair_terms = cin_pairs(embedded).astype(jnp.bfloat16)
    pair_total = jnp.sum(pair_terms.astype(jnp.float32), axis=1)
    grad_cin_u = jnp.dot(grad_logits, stored[0], precision=highest)
    grad_maps = (grad_logits[:, None] * cin_u.astype(jnp.float32)[None, :]).astype(jnp.bfloat16)
    grad_cin_w = lax.dot_general(
        grad_maps.astype(jnp.float32),
        pair_total,
        (((0,), (0,)), ((), ())),
        precision=highest,
        preferred_element_type=jnp.float32,
    )
    grad_pairs = jnp.dot(grad_maps, cin_w, preferred_element_type=jnp.float32).reshape(
        samples, FIELDS, FIELDS
    )
    symmetric = grad_pairs + jnp.swapaxes(grad_pairs, 1, 2)
    grad_embed = jnp.einsum("sij,sjd->sid", symmetric, embedded, precision=highest)
    grad_part = jnp.concatenate([grad_embed, jnp.zeros((samples, FIELDS, 1), jnp.float32)], axis=2)
    gradients = [grad_cin_w, grad_cin_u] + [
        jnp.zeros(piece.shape, jnp.float32) for piece in params[2:]
    ]
    return (grad_part, pack(gradients, total_size))


def deep_backward(pooled, grad_logits, stored, params, total_size):
    cin_w, cin_u, w_one, b_one, w_two, b_two, w_three, bias = params
    unused, pre_one, pre_two = stored
    samples = pooled.shape[0]
    flat_embed = pooled[:, :, :EMB].reshape(samples, FIELDS * EMB).astype(jnp.bfloat16)
    grad_w_three = jnp.dot(grad_logits, jax.nn.relu(pre_two), precision=highest)
    grad_pre_two = jnp.where(
        pre_two > 0, grad_logits[:, None] * w_three.astype(jnp.float32)[None, :], 0.0
    ).astype(jnp.bfloat16)
    hidden_one = jax.nn.relu(pre_one).astype(jnp.bfloat16)
    grad_w_two = lax.dot_general(
        hidden_one, grad_pre_two, (((0,), (0,)), ((), ())), preferred_element_type=jnp.float32
    )
    grad_b_two = jnp.sum(grad_pre_two.astype(jnp.float32), axis=0)
    grad_hidden = lax.dot_general(
        grad_pre_two, w_two, (((1,), (1,)), ((), ())), preferred_element_type=jnp.float32
    )
    grad_pre_one = jnp.where(pre_one > 0, grad_hidden, 0.0).astype(jnp.bfloat16)
    grad_w_one = lax.dot_general(
        flat_embed, grad_pre_one, (((0,), (0,)), ((), ())), preferred_element_type=jnp.float32
    )
    grad_b_one = jnp.sum(grad_pre_one.astype(jnp.float32), axis=0)
    grad_flat = lax.dot_general(
        grad_pre_one, w_one, (((1,), (1,)), ((), ())), preferred_element_type=jnp.float32
    )
    grad_linear = jnp.broadcast_to(grad_logits[:, None, None], (samples, FIELDS, 1))
    grad_part = jnp.concatenate([grad_flat.reshape(samples, FIELDS, EMB), grad_linear], axis=2)
    gradients = [
        jnp.zeros(cin_w.shape, jnp.float32),
        jnp.zeros(cin_u.shape, jnp.float32),
        grad_w_one,
        grad_b_one,
        grad_w_two,
        grad_b_two,
        grad_w_three,
        jnp.sum(grad_logits)[None],
    ]
    return (grad_part, pack(gradients, total_size))


def shards(
    shard_ids,
    local_rows,
    bag_counts,
    click_labels,
    sample_weights,
    embed_table,
    table_first,
    table_second,
    dense_params,
    dense_first,
    dense_second,
):
    tower_count = lax.axis_size("tower")
    batch_count = lax.axis_size("batch")
    tower_at = lax.axis_index("tower")
    micro_count = shard_ids.shape[0]
    samples = shard_ids.shape[1]
    rows_dev = embed_table.shape[1]
    capacity = 4 * samples * IDS_SAMP // (tower_count * batch_count)
    total_size = dense_params.shape[0] * tower_count * batch_count
    whole = lax.all_gather(
        dense_params.astype(jnp.bfloat16), ("tower", "batch"), axis=0, tiled=True
    )
    params = unpack(whole)
    table_low = embed_table.astype(jnp.bfloat16)
    total_weight = lax.psum(jnp.sum(sample_weights.astype(jnp.float32)), "batch")
    owners = shard_ids.reshape(micro_count, samples * IDS_SAMP)
    wanted_rows = local_rows.reshape(micro_count, samples * IDS_SAMP)
    slots, sources, valids = jax.vmap(
        lambda owner_ids: place_ids(owner_ids, tower_at, batch_count, capacity)
    )(owners)
    requests = jnp.where(
        valids,
        jnp.take_along_axis(wanted_rows, sources.reshape(micro_count, -1), axis=1).reshape(
            sources.shape
        ),
        -1,
    )
    dense_grad = jnp.zeros((total_size,), jnp.float32)
    loss_part = jnp.zeros((), jnp.float32)
    arrived = []
    served_list = []
    for index_micro in range(micro_count):
        answer_one, served_one = lookup(requests[index_micro : index_micro + 1], table_low)
        answer = answer_one[0]
        columns = answer.shape[-1]
        stacked = jnp.concatenate(
            [answer.reshape(-1, columns), jnp.zeros((1, columns), jnp.bfloat16)], axis=0
        )
        picked = stacked[slots[index_micro]].reshape(samples, IDS_SAMP, columns)
        fields = field_table(bag_counts[index_micro])
        pooled_part = jnp.einsum(
            "skf,skc->sfc", fields.astype(jnp.bfloat16), picked, preferred_element_type=jnp.float32
        )
        pooled = lax.psum(pooled_part, "tower")
        logit_part, stored = lax.cond(tower_at == 0, cin_forward, deep_forward, pooled, params)
        logits = lax.psum(logit_part, "tower")
        weight_here = sample_weights[index_micro].astype(jnp.float32)
        label_here = click_labels[index_micro].astype(jnp.float32)
        loss_part = loss_part + jnp.sum(
            weight_here * (jax.nn.softplus(logits) - label_here * logits)
        )
        grad_logits = weight_here * (jax.nn.sigmoid(logits) - label_here) / total_weight
        grad_part, grad_flat = lax.cond(
            tower_at == 0,
            partial(cin_backward, total_size=total_size),
            partial(deep_backward, total_size=total_size),
            pooled,
            grad_logits,
            stored,
            params,
        )
        dense_grad = dense_grad + grad_flat
        grad_pooled = lax.psum(grad_part.astype(jnp.bfloat16), "tower").astype(jnp.float32)
        per_id = jnp.einsum("skf,sfc->skc", fields, grad_pooled, precision=highest).reshape(
            -1, columns
        )
        sendable = jnp.where(valids[index_micro][..., None], per_id[sources[index_micro]], 0.0)
        sendable = sendable.reshape(1, batch_count, capacity, columns)
        arrived.append(deliver(sendable))
        served_list.append(served_one)
    table_grad = scatter_rows(
        jnp.concatenate(arrived, axis=0), jnp.concatenate(served_list, axis=0), rows_dev
    )
    shaped = dense_grad.reshape(tower_count, batch_count, -1)
    within_group = lax.psum_scatter(shaped, "batch", scatter_dimension=1, tiled=True)
    own_grad = lax.psum_scatter(within_group, "tower", scatter_dimension=0, tiled=True).reshape(-1)
    table_new, table_first_new, table_second_new = adam_update(
        embed_table, table_first, table_second, table_grad, rate_table
    )
    dense_new, dense_first_new, dense_second_new = adam_update(
        dense_params, dense_first, dense_second, own_grad, rate_dense
    )
    loss_sum = lax.psum(loss_part, "batch") / total_weight
    return (
        table_new,
        table_first_new,
        table_second_new,
        table_new.astype(jnp.bfloat16),
        dense_new,
        dense_first_new,
        dense_second_new,
        dense_new.astype(jnp.bfloat16),
        loss_sum,
    )


def solution(mesh):
    placed = (
        P(None, "batch", None, None),
        P(None, "batch", None, None),
        P(None, "batch", None),
        P(None, "batch"),
        P(None, "batch"),
        P(None, ("tower", "batch")),
        P(None, ("tower", "batch")),
        P(None, ("tower", "batch")),
        P(("tower", "batch")),
        P(("tower", "batch")),
        P(("tower", "batch")),
    )
    return jax.shard_map(
        shards,
        mesh=mesh,
        in_specs=placed,
        out_specs=(
            P(None, ("tower", "batch")),
            P(None, ("tower", "batch")),
            P(None, ("tower", "batch")),
            P(None, ("tower", "batch")),
            P(("tower", "batch")),
            P(("tower", "batch")),
            P(("tower", "batch")),
            P(("tower", "batch")),
            P(),
        ),
        check_vma=False,
    )
```

profile of v0, /device:TPU:0, one launch (start us, length us, event | category | flops | bytes accessed | tf_op | source)
XLA Modules:
  0.0 1850.0 jit_solution(15249911199826438598)
XLA Ops:
  26.1 7.6 copy.406
  34.3 354.2 %gather_fusion.6 = s32[49920]{0:T(1024)S(1)} fusion(s32[3,8320]{1,0:T(4,128)} %get-tuple-element.227, s32[49920]{0:T(1024)S(1)} %reshape.689), kind=kCustom, calls=%fused_computation.9 | custom fusion | bytes 798720 | tf_op jit(solution)/shard_map/vmap()/gather | solution.py:101
  389.3 400.4 %gather_fusion.7 = s32[49920]{0:T(1024)S(1)} fusion(s32[3,8320]{1,0:T(4,128)S(1)} %reshape.599, s32[49920]{0:T(1024)S(1)} %reshape.695), kind=kCustom, calls=%fused_computation.10 | custom fusion | bytes 798720 | tf_op jit(solution)/shard_map/jit(take_along_axis)/gather | solution.py:258
  790.7 8.3 all-to-all-start
  810.1 7.5 all-to-all-done.2
  821.3 7.3 all-to-all-done.1
  828.8 35.5 %gather_fusion.9 = bf16[16640,11]{1,0:T(8,128)(2,1)} fusion(bf16[11,32768]{0,1:T(8,128)(2,1)} %copy.406, s32[17408]{0:T(1024)S(1)} %pad_clamp_fusion.3), kind=kCustom, calls=%fused_computation.1.clone | custom fusion | bytes 798720 | tf_op jit(solution)/shard_map/jit(_take)/gather | solution.py:109
  873.2 35.5 %gather_fusion.10 = bf16[16640,11]{1,0:T(8,128)(2,1)} fusion(bf16[11,32768]{0,1:T(8,128)(2,1)} %copy.406, s32[17408]{0:T(1024)S(1)} %pad_clamp_fusion.1), kind=kCustom, calls=%fused_computation.2.clone | custom fusion | bytes 798720 | tf_op jit(solution)/shard_map/jit(_take)/gather | solution.py:109
  920.7 35.5 %gather_fusion.8 = bf16[16640,11]{1,0:T(8,128)(2,1)} fusion(bf16[11,32768]{0,1:T(8,128)(2,1)} %copy.406, s32[17408]{0:T(1024)S(1)} %pad_clamp_fusion.5), kind=kCustom, calls=%fused_computation.clone | custom fusion | bytes 798720 | tf_op jit(solution)/shard_map/jit(_take)/gather | solution.py:109
  979.1 16.6 gather_fusion.2
  1015.1 16.6 gather_fusion.4
  1031.8 19.0 %gather_fusion = bf16[8320,11]{1,0:T(8,128)(2,1)} fusion(bf16[16641,11]{1,0:T(8,128)(2,1)} %concatenate.56, s32[9216]{0:T(1024)S(1)} %copy-done.26), kind=kCustom, calls=%fused_computation.3 | custom fusion | bytes 399360 | tf_op jit(solution)/shard_map/gather | solution.py:274
  1061.1 16.4 all-reduce.25.cloned.1.call-done
  1078.6 15.0 conditional.8
  1094.9 16.2 conditional.6
  1111.6 18.1 conditional.10
  1136.4 42.4 %all-reduce.9 = (f32[]{:T(128)}, f32[]{:T(128)}) all-reduce(f32[]{:T(128)} %convert_reduce_fusion.14, f32[]{:T(128)S(6)} %add.386), channel_id=1, replica_groups=mesh['tower'=2,'batch'=16] {'batch'}, use_global_device_ids=true, to_apply=%region_15.17 | all-reduce | flops 2 | bytes 16 | tf_op jit(solution)/shard_map/psum | solution.py:250
  1179.5 61.2 %conditional.9 = (bf16[104,39,11]{0,2,1:T(8,128)(2,1)}, f32[621632]{0:T(1024)}) conditional(s32[]{:T(128)} %convert_element_type.328, (f32[104,400]{0,1:T(8,128)}, f32[104,400]{0,1:T(8,128)}, f32[104]{0:T(128)S(1)}, bf16[400]{0:T(512)(128)(2,1)S(1)}, bf16[400,400]{1,0:T(8,128)(2,1)S(1)}, /*index=5*/bf16[390,400]{1,0:T(8,128)(2,1)S(1)}, ...), branch_computations={%region_31.36_spmd, %region_35.38_spmd} | conditional | flops 468557632 | bytes 19585076 | solution.py:288
  1204.0 25.6 %concatenate.43 = f32[621632]{0:T(1024)} concatenate(f32[304200]{0:T(1024)} %reshape.575, f32[200]{0:T(256)S(1)} %bitcast.376, f32[156000]{0:T(1024)} %broadcast.484, f32[400]{0:T(512)S(1)} %broadcast.485, f32[160000]{0:T(1024)} %broadcast.486, f32[800]{0:T(1024)S(1)} %broadcast.487, f32[1]{0:T(128)} %constant.93.clone, f32[31]{0:T(128)S(1)} %broadcast.488), dimensions={0} | concatenate | bytes 4973056 | tf_op jit(solution)/shard_map/cond/branch_1_fun/concatenate | solution.py:76
  1242.2 52.5 %conditional.7 = (bf16[104,39,11]{0,2,1:T(8,128)(2,1)}, f32[621632]{0:T(1024)}) conditional(s32[]{:T(128)} %convert_element_type.328, (f32[104,400]{0,1:T(8,128)}, f32[104,400]{0,1:T(8,128)}, f32[104]{0:T(128)S(1)}, bf16[400]{0:T(512)(128)(2,1)S(1)}, bf16[400,400]{1,0:T(8,128)(2,1)S(1)}, /*index=5*/bf16[390,400]{1,0:T(8,128)(2,1)S(1)}, ...), branch_computations={%region_16.21_spmd, %region_20.23_spmd} | conditional | flops 468557632 | bytes 22116048 | solution.py:288
  1260.8 25.7 %concatenate.39 = f32[621632]{0:T(1024)} concatenate(f32[304200]{0:T(1024)} %reshape.570, f32[200]{0:T(256)S(1)} %bitcast.377, f32[156000]{0:T(1024)} %broadcast.471, f32[400]{0:T(512)S(1)} %broadcast.472, f32[160000]{0:T(1024)} %broadcast.473, f32[800]{0:T(1024)S(1)} %broadcast.474, f32[1]{0:T(128)} %constant.82.clone, f32[31]{0:T(128)S(1)} %broadcast.475), dimensions={0} | concatenate | bytes 4973056 | tf_op jit(solution)/shard_map/cond/branch_1_fun/concatenate | solution.py:76
  1296.4 41.5 %conditional.11 = (bf16[104,39,11]{0,2,1:T(8,128)(2,1)}, f32[621632]{0:T(1024)S(1)}) conditional(s32[]{:T(128)} %convert_element_type.328, (f32[104,400]{0,1:T(8,128)}, f32[104,400]{0,1:T(8,128)}, f32[104]{0:T(128)S(1)}, bf16[400]{0:T(512)(128)(2,1)S(1)}, bf16[400,400]{1,0:T(8,128)(2,1)S(1)}, /*index=5*/bf16[390,400]{1,0:T(8,128)(2,1)S(1)}, ...), branch_computations={%region_46.51_spmd, %region_50.53_spmd} | conditional | flops 468557632 | bytes 19585076 | solution.py:288
  1306.6 20.2 %concatenate.47 = f32[621632]{0:T(1024)S(1)} concatenate(f32[304200]{0:T(1024)} %reshape.580, f32[200]{0:T(256)S(1)} %bitcast.378, f32[156000]{0:T(1024)} %broadcast.497, f32[400]{0:T(512)S(1)} %broadcast.498, f32[160000]{0:T(1024)} %broadcast.499, f32[800]{0:T(1024)S(1)} %broadcast.500, f32[1]{0:T(128)} %constant.103.clone, f32[31]{0:T(128)S(1)} %broadcast.501), dimensions={0} | concatenate | bytes 4973056 | tf_op jit(solution)/shard_map/cond/branch_1_fun/concatenate | solution.py:76
  1359.5 34.0 %gather_fusion.5 = bf16[16640,11]{1,0:T(8,128)(2,1)} fusion(bf16[8320,11]{1,0:T(8,128)(2,1)S(1)} %bitcast.350, s32[17408]{0:T(1024)S(1)} %copy-done.23), kind=kCustom, calls=%fused_computation.8 | custom fusion | bytes 798720 | tf_op jit(solution)/shard_map/gather | solution.py:302
  1398.3 7.0 all-to-all-start.8
  1406.7 34.0 %gather_fusion.3 = bf16[16640,11]{1,0:T(8,128)(2,1)} fusion(bf16[8320,11]{1,0:T(8,128)(2,1)S(1)} %bitcast.351, s32[17408]{0:T(1024)S(1)} %copy-done.24), kind=kCustom, calls=%fused_computation.6 | custom fusion | bytes 798720 | tf_op jit(solution)/shard_map/gather | solution.py:302
  1454.7 37.0 %gather_fusion.1 = bf16[16640,11]{1,0:T(8,128)(2,1)} fusion(bf16[8320,11]{1,0:T(8,128)(2,1)S(1)} %bitcast.352, s32[17408]{0:T(1024)} %pad_clamp_fusion.4), kind=kCustom, calls=%fused_computation.4 | custom fusion | bytes 798720 | tf_op jit(solution)/shard_map/gather | solution.py:302
  1509.3 9.8 all-to-all-done.4
  1520.6 14.4 copy.476
  1534.9 274.1 %scatter_custom_fusion = f32[11,32768]{0,1:T(8,128)} fusion(s32[49920]{0:T(1024)S(1)} %fusion.111, f32[49920,11]{1,0:T(8,128)} %bitcast.353, f32[]{:T(128)} %constant.105.clone.1), kind=kCustom, calls=%fused_computation.162 | custom fusion | flops 549120 | bytes 1442304 | tf_op jit(solution)/shard_map/scatter-add | solution.py:125
  1809.0 11.0 copy.458
  1829.4 9.2 all-reduce.23.cloned.1.call-done
  (346 shorter events, 322.7 us)
Async XLA Ops:
  8.0 26.3 %sort.19.cloned.1.call-start = ((), (), s32[]{:S(2)}) async-start(), calls=%async_computation.14 | async-start | bytes 798752 | tf_op jit(solution)/shard_map/vmap(jit(argsort))/sort | solution.py:98
  15.2 1040.1 %all-reduce.19.cloned.1.call-start = ((), (), s32[]{:S(2)}) async-start(), calls=%async_computation.9 | async-start | bytes 2490368
  389.3 400.6 %copy-start.37 = (s32[3,17]{1,0:T(4,128)S(1)}, s32[3,17]{1,0:T(4,128)}, u32[]{:S(2)}) copy-start(s32[3,17]{1,0:T(4,128)} %copy-done.36) | copy-start | bytes 616
  790.7 15.9 all-to-all-start
  806.6 11.0 all-to-all-start.2
  817.6 11.0 all-to-all-start.1
  828.7 39.5 %copy-start.10 = (s32[1,16,1040]{2,0,1:T(1,128)}, s32[1,16,1040]{2,0,1:T(1,128)S(1)}, u32[]{:S(2)}) copy-start(s32[1,16,1040]{2,0,1:T(1,128)S(1)} %all-to-all-done.1) | copy-start | bytes 199684
  869.3 44.4 %all-to-all-start.5 = ((bf16[1,16,1040,11]{2,3,0,1:T(8,128)(2,1)}), bf16[1,16,1040,11]{2,3,0,1:T(8,128)(2,1)S(1)}, u32[]{:S(2)}, u32[]{:S(2)}) async-start(bf16[1,16,1040,11]{2,3,0,1:T(8,128)(2,1)} %fusion.102), calls=%async_computation.5 | async-start | bytes 1179648 | tf_op jit(solution)/shard_map/all_to_all | solution.py:111
  913.7 47.5 %all-to-all-start.7 = ((bf16[1,16,1040,11]{2,3,0,1:T(8,128)(2,1)}), bf16[1,16,1040,11]{2,3,0,1:T(8,128)(2,1)S(1)}, u32[]{:S(2)}, u32[]{:S(2)}) async-start(bf16[1,16,1040,11]{2,3,0,1:T(8,128)(2,1)} %fusion.100), calls=%async_computation.7 | async-start | bytes 1179648 | tf_op jit(solution)/shard_map/all_to_all | solution.py:111
  961.1 45.1 %all-to-all-start.3 = ((bf16[1,16,1040,11]{2,3,0,1:T(8,128)(2,1)}), bf16[1,16,1040,11]{2,3,0,1:T(8,128)(2,1)S(1)}, u32[]{:S(2)}, u32[]{:S(2)}) async-start(bf16[1,16,1040,11]{2,3,0,1:T(8,128)(2,1)} %fusion.104), calls=%async_computation.3 | async-start | bytes 1179648 | tf_op jit(solution)/shard_map/all_to_all | solution.py:111
  968.0 109.4 %all-reduce.25.cloned.1.call-start = ((), (), s32[]{:S(2)}) async-start(), calls=%async_computation.12 | async-start | bytes 5111808 | tf_op jit(solution)/shard_map/psum | solution.py:279
  979.1 16.7 copy-start.16
  1015.1 16.7 copy-start.26
  1031.8 19.1 %copy-start.18 = (s32[104,80]{1,0:T(8,128)S(1)}, s32[104,80]{1,0:T(8,128)}, u32[]{:S(2)}) copy-start(s32[104,80]{1,0:T(8,128)} %copy.439) | copy-start | bytes 99844
  1054.2 299.5 %all-reduce.27.cloned.1.call-start = ((), (), s32[]{:S(2)}) async-start(), calls=%async_computation.13 | async-start | bytes 675840 | tf_op jit(solution)/shard_map/psum | solution.py:298
  1059.4 34.3 %copy-start.3 = (bf16[200,1521]{1,0:T(8,128)(2,1)}, bf16[200,1521]{1,0:T(8,128)(2,1)S(1)}, u32[]{:S(2)}) copy-start(bf16[200,1521]{1,0:T(8,128)(2,1)S(1)} %reshape.604) | copy-start | bytes 1825204
  1061.0 50.1 %copy-start.44 = (bf16[200]{0:T(256)(128)(2,1)}, bf16[200]{0:T(256)(128)(2,1)S(1)}, u32[]{:S(2)}) copy-start(bf16[200]{0:T(256)(128)(2,1)S(1)} %slice.220) | copy-start | bytes 1204
  1111.1 21.2 %copy-start.39 = (s32[3,104]{1,0:T(4,128)S(1)}, s32[3,104]{1,0:T(4,128)}, u32[]{:S(2)}) copy-start(s32[3,104]{1,0:T(4,128)} %param.29) | copy-start | bytes 3748
  1111.1 21.2 %copy-start.40 = (s32[3,104]{1,0:T(4,128)S(1)}, s32[3,104]{1,0:T(4,128)}, u32[]{:S(2)}) copy-start(s32[3,104]{1,0:T(4,128)} %param.28) | copy-start | bytes 3748
  1111.1 68.4 %copy-start.2 = (f32[104,39,11]{1,2,0:T(8,128)S(1)}, f32[104,39,11]{1,2,0:T(8,128)}, u32[]{:S(2)}) copy-start(f32[104,39,11]{1,2,0:T(8,128)} %get-tuple-element.696) | copy-start | bytes 535396
  1260.8 25.7 %copy-start.8 = (f32[104,39,39]{0,2,1:T(8,128)S(1)}, f32[104,39,39]{0,2,1:T(8,128)}, u32[]{:S(2)}) copy-start(f32[104,39,39]{0,2,1:T(8,128)} %bitcast_add_fusion) | copy-start | bytes 1898212 | tf_op jit(solution)/shard_map/cond
  1339.5 480.5 %all-reduce.21.cloned.1.call-start = ((), (), s32[]{:S(2)}) async-start(), calls=%async_computation.10 | async-start | bytes 4980736
  1398.3 47.2 %all-to-all-start.8 = ((bf16[1,16,1040,11]{2,3,0,1:T(8,128)(2,1)}), bf16[1,16,1040,11]{2,3,0,1:T(8,128)(2,1)S(1)}, u32[]{:S(2)}, u32[]{:S(2)}) async-start(bf16[1,16,1040,11]{2,3,0,1:T(8,128)(2,1)} %select_convert_fusion.3), calls=%async_computation.8 | async-start | bytes 1179648 | tf_op jit(solution)/shard_map/all_to_all | solution.py:116
  1445.5 51.1 %all-to-all-start.6 = ((bf16[1,16,1040,11]{2,3,0,1:T(8,128)(2,1)}), bf16[1,16,1040,11]{2,3,0,1:T(8,128)(2,1)S(1)}, u32[]{:S(2)}, u32[]{:S(2)}) async-start(bf16[1,16,1040,11]{2,3,0,1:T(8,128)(2,1)} %select_convert_fusion.4), calls=%async_computation.6 | async-start | bytes 1179648 | tf_op jit(solution)/shard_map/all_to_all | solution.py:116
  1495.6 8.9 copy-start.42
  1495.6 9.5 copy-start.11
  1496.6 22.5 %all-to-all-start.4 = ((bf16[1,16,1040,11]{2,3,0,1:T(8,128)(2,1)}), bf16[1,16,1040,11]{2,3,0,1:T(8,128)(2,1)S(1)}, u32[]{:S(2)}, u32[]{:S(2)}) async-start(bf16[1,16,1040,11]{2,3,0,1:T(8,128)(2,1)} %select_convert_fusion.5), calls=%async_computation.4 | async-start | bytes 1179648 | tf_op jit(solution)/shard_map/all_to_all | solution.py:116
  1503.5 335.1 %all-reduce.23.cloned.1.call-start = ((), (), s32[]{:S(2)}) async-start(), calls=%async_computation.11 | async-start | bytes 311296
  1809.0 13.4 copy-start.5
  1822.4 17.8 copy-start.22
  1822.4 17.8 copy-start.30
  1822.4 17.8 copy-start.31
  (27 other events, 116.9 us)
Sparse Core Ops, SparseCore 0:
  15.3 6.7 sort.21.cloned.1.call-done
  (1 shorter events, 0.0 us)
Sparse Core Ops, SparseCore 1:
  21.7 132.9 all-reduce.18
  1054.2 23.2 all-reduce.24
  1339.6 14.0 all-reduce.26
  1360.2 140.3 all-reduce.20
  1822.5 16.1 all-reduce.22
where the time goes:
time: 1860 us; the launch traced here: 1850 us
  local copies, waits for them, and re-layouts  1290 us (69%)
  other arithmetic  326 us (18%)
  waiting for transfers between devices  59.4 us (3%)
  starting transfers between devices  55.2 us (3%)
  matrix products  53.2 us (3%)
  blocking collectives  45 us (2%)
  between operations  21.4 us (1%)
    gather x3, local copies, waits for them, and re-layouts, shards(): jnp.take_along_axis(wanted_rows, sources.reshape(micro_count, -1), axis=1)  401 us
    gather x3, local copies, waits for them, and re-layouts, place_ids(): source = ordering[jnp.minimum(starts[:, None] + within, id_count - 1)]  354 us
    scatter-add x1, other arithmetic, scatter_rows(): jnp.zeros((columns, rows_dev), jnp.float32).at[:, places]  274 us
    gather x6, local copies, waits for them, and re-layouts, lookup(): jnp.take(table_low, jnp.maximum(wanted, 0), axis=1)  118 us
    gather x6, local copies, waits for them, and re-layouts, shards(): per_id[sources[index_micro]]  117 us
    concatenate x3, local copies, waits for them, and re-layouts, pack(): jnp.concatenate([flat_grad, jnp.zeros((total_size - flat_grad.shape[0],),...  71.5 us
    gather x3, local copies, waits for them, and re-layouts, shards(): picked = stacked[slots[index_micro]].reshape(samples, IDS_SAMP, columns)  52.3 us
    psum x1, blocking collectives, shards(): lax.psum(jnp.sum(sample_weights.astype(jnp.float32)), 'batch')  42.4 us
  transfers between devices with their start and end apart: 14, of which 7 were waited for; matrix products, arithmetic and copies ran while one was open for 78% of the time, Pallas kernels for 0%

commit v1 on v0

v1 whole, which is shorter than its diff:
```python
from functools import partial

import jax
import jax.numpy as jnp
from jax import lax
from jax.experimental import pallas as pl
from jax.experimental.pallas import tpu as pltpu
from jax.sharding import PartitionSpec as P

FIELDS = 39
EMB = 10
MAPS = 200
HID = 400
IDS_SAMP = 80

beta_one = 0.9
beta_two = 0.999
epsilon = 1e-08
decay_rate = 0.15
rate_table = 0.1
rate_dense = 0.05
step_count = 10

LANES = 128
WIDE = 256
HALF = 24
BAG_ROWS = EMB * HALF + 8
FPAD = 40
PAIRS = FIELDS * FPAD
NT = (((1,), (1,)), ((), ()))
TN = (((0,), (0,)), ((), ()))
NN = (((1,), (0,)), ((), ()))


def adam_update(weight, first_old, second_old, gradient, step_rate):
    first_new = beta_one * first_old + (1.0 - beta_one) * gradient
    second_new = beta_two * second_old + (1.0 - beta_two) * gradient * gradient
    first_hat = first_new / (1.0 - beta_one**step_count)
    second_hat = second_new / (1.0 - beta_two**step_count)
    weight_new = weight - step_rate * (
        first_hat / (jnp.sqrt(second_hat) + epsilon) + decay_rate * weight
    )
    return (weight_new, first_new, second_new)


def dot(a, b, dims=NN):
    return lax.dot_general(a, b, dims, preferred_element_type=jnp.float32)


def iota(shape, dim):
    return lax.broadcasted_iota(jnp.int32, shape, dim)


def ones_at(mask):
    return jnp.where(mask, 1.0, 0.0).astype(jnp.bfloat16)


def layout_of(micro_count, capacity):
    first_rows = [m * capacity // WIDE for m in range(micro_count)]
    shifts = [m * capacity % WIDE for m in range(micro_count)]
    window = max(-(-(shift + capacity) // WIDE) for shift in shifts)
    return first_rows, shifts, window, max(first_rows) + window


def route_kernel(
    capacity, batch_count, micro_count, ids_ref, rows_ref, lanes_ref, field_ref,
    req_ref, code_ref, half_ref, slot_ref, left_ref, right_ref,
):
    first_rows, shifts, window, rows_msg = layout_of(micro_count, capacity)
    micro = pl.program_id(0)
    id_rows = ids_ref.shape[1]
    chunk = 16
    target = ids_ref[0]

    @pl.when(micro == 0)
    def _():
        req_ref[...] = jnp.zeros_like(req_ref)
        code_ref[...] = jnp.zeros_like(code_ref)
        half_ref[...] = jnp.zeros_like(half_ref)

    earlier_rows = ones_at(iota((id_rows, id_rows), 1) < iota((id_rows, id_rows), 0))
    upper = iota((2 * LANES, LANES), 0)
    mixing = ones_at((upper < iota((2 * LANES, LANES), 1)) | (upper >= LANES))
    rank = jnp.zeros((id_rows, LANES), jnp.float32)
    for begin in range(0, batch_count, chunk):
        hots = [ones_at(target == begin + d) for d in range(chunk)]
        above = dot(earlier_rows, jnp.concatenate(hots, axis=1)).astype(jnp.bfloat16)
        stacked = jnp.concatenate(
            [
                jnp.concatenate([hots[d], above[:, d * LANES : (d + 1) * LANES]], axis=1)
                for d in range(chunk)
            ],
            axis=0,
        )
        ranks = dot(stacked, mixing)
        for d in range(chunk):
            rank = rank + jnp.where(
                target == begin + d, ranks[d * id_rows : (d + 1) * id_rows], 0.0
            )
    shift = sum(jnp.where(micro == m, shifts[m], 0) for m in range(micro_count))
    place = rank.astype(jnp.int32) + shift
    slot_ref[0] = jnp.where(target < batch_count, (place // WIDE) * batch_count + target, -1)
    slot_ref[1] = place % WIDE
    places = window * batch_count

    def build(t, carry):
        here = pl.ds(t, 1)
        span = pl.ds(pl.multiple_of(t * LANES, LANES), LANES)
        mask = iota((places, LANES), 0) == slot_ref[0, here, :]
        row = rows_ref[0, here, :]
        values = [row // LANES, row % LANES, lanes_ref[0, here, :] + 1, field_ref[0, here, :]]
        for v in range(4):
            value = values[v].astype(jnp.float32)
            left_ref[v * places : (v + 1) * places, span] = jnp.where(mask, value, 0.0).astype(
                jnp.bfloat16
            )
        right_ref[:, span] = ones_at(iota((WIDE, LANES), 0) == slot_ref[1, here, :])
        return carry

    lax.fori_loop(0, id_rows, build, 0)
    placed = dot(left_ref[...], right_ref[...], NT)

    def part(v, r):
        return placed[(v * window + r) * batch_count : (v * window + r + 1) * batch_count].astype(
            jnp.int32
        )

    for m in range(micro_count):

        @pl.when(micro == m)
        def _():
            for r in range(window):
                code = part(2, r)
                at = first_rows[m] + r
                req_ref[at] += part(0, r) * LANES + part(1, r)
                code_ref[at] += jnp.where(code > 0, code + m * WIDE, 0)
                half_ref[at] += part(3, r)


def route(targets, rows, lane_codes, half_fields, capacity, batch_count):
    micro_count, id_rows, _ = targets.shape
    _, _, window, rows_msg = layout_of(micro_count, capacity)
    block = pl.BlockSpec((1, id_rows, LANES), lambda m: (m, 0, 0))
    whole = pl.BlockSpec((rows_msg, batch_count, WIDE), lambda m: (0, 0, 0))
    shape = jax.ShapeDtypeStruct((rows_msg, batch_count, WIDE), jnp.int32)
    return pl.pallas_call(
        partial(route_kernel, capacity, batch_count, micro_count),
        grid=(micro_count,),
        in_specs=[block] * 4,
        out_specs=[whole] * 3,
        out_shape=[shape] * 3,
        scratch_shapes=[
            pltpu.VMEM((2, id_rows, LANES), jnp.int32),
            pltpu.VMEM((4 * window * batch_count, id_rows * LANES), jnp.bfloat16),
            pltpu.VMEM((WIDE, id_rows * LANES), jnp.bfloat16),
        ],
        compiler_params=pltpu.CompilerParams(vmem_limit_bytes=60 << 20),
        name="route",
    )(targets, rows, lane_codes, half_fields)


def gather_columns(result, mask, depth, columns):
    width = result.shape[1]
    out = jnp.zeros((16, width), jnp.float32)
    for c in range(columns):
        row = jnp.sum(
            jnp.where(mask, result[c * depth : (c + 1) * depth], 0.0), axis=0, keepdims=True
        )
        out = jnp.where(iota((16, width), 0) == c, row, out)
    return out


def lookup_kernel(columns, req_ref, table_ref, out_ref):
    tiles = table_ref.shape[1]

    def step(r, carry):
        row = req_ref[0, pl.ds(r, 1), :]
        hot = ones_at(iota((tiles, WIDE), 0) == row // LANES)
        result = dot(table_ref[...], hot)
        mask = iota((LANES, WIDE), 0) == row % LANES
        span = pl.ds(pl.multiple_of(r * WIDE, WIDE), WIDE)
        out_ref[0, :, span] = gather_columns(result, mask, LANES, columns).astype(jnp.bfloat16)
        return carry

    lax.fori_loop(0, req_ref.shape[1], step, 0)


def lookup(requests, table_tiles):
    batch_count, rows_msg, _ = requests.shape
    columns = table_tiles.shape[0] // LANES
    return pl.pallas_call(
        partial(lookup_kernel, columns),
        grid=(batch_count,),
        in_specs=[
            pl.BlockSpec((1, rows_msg, WIDE), lambda d: (d, 0, 0)),
            pl.BlockSpec(table_tiles.shape, lambda d: (0, 0)),
        ],
        out_specs=pl.BlockSpec((1, 16, rows_msg * WIDE), lambda d: (d, 0, 0)),
        out_shape=jax.ShapeDtypeStruct((batch_count, 16, rows_msg * WIDE), jnp.bfloat16),
        compiler_params=pltpu.CompilerParams(vmem_limit_bytes=60 << 20),
        name="lookup",
    )(requests, table_tiles)


def pool_kernel(capacity, micro_count, ans_ref, code_ref, half_ref, out_ref, left_ref):
    first_rows, _, window, rows_msg = layout_of(micro_count, capacity)

    @pl.when(pl.program_id(0) == 0)
    def _():
        out_ref[...] = jnp.zeros_like(out_ref)

    for r in range(rows_msg):
        span = slice(r * WIDE, (r + 1) * WIDE)
        values = ans_ref[0, :, span].astype(jnp.float32)
        mask = iota((HALF, WIDE), 0) == half_ref[0, r : r + 1, :]
        pieces = [jnp.where(mask, values[c : c + 1], 0.0) for c in range(EMB)]
        pieces.append(jnp.where(iota((8, WIDE), 0) == 0, values[EMB : EMB + 1], 0.0))
        left_ref[:, span] = jnp.concatenate(pieces, axis=0).astype(jnp.bfloat16)
    for m in range(micro_count):
        rights = [
            ones_at(iota((WIDE, WIDE), 0) + (m * WIDE + 1) == code_ref[0, r : r + 1, :])
            for r in range(first_rows[m], first_rows[m] + window)
        ]
        span = slice(first_rows[m] * WIDE, (first_rows[m] + window) * WIDE)
        out_ref[m] += dot(left_ref[:, span], jnp.concatenate(rights, axis=1), NT)


def pool(answers, codes, halves, capacity, micro_count):
    batch_count, rows_msg, _ = codes.shape
    block = pl.BlockSpec((1, rows_msg, WIDE), lambda d: (d, 0, 0))
    return pl.pallas_call(
        partial(pool_kernel, capacity, micro_count),
        grid=(batch_count,),
        in_specs=[pl.BlockSpec((1, 16, rows_msg * WIDE), lambda d: (d, 0, 0)), block, block],
        out_specs=pl.BlockSpec((micro_count, BAG_ROWS, WIDE), lambda d: (0, 0, 0)),
        out_shape=jax.ShapeDtypeStruct((micro_count, BAG_ROWS, WIDE), jnp.float32),
        scratch_shapes=[pltpu.VMEM((BAG_ROWS, rows_msg * WIDE), jnp.bfloat16)],
        compiler_params=pltpu.CompilerParams(vmem_limit_bytes=60 << 20),
        name="pool",
    )(answers, codes, halves)


def spread_kernel(capacity, micro_count, grad_ref, code_ref, half_ref, out_ref):
    first_rows, _, window, rows_msg = layout_of(micro_count, capacity)
    for r in range(rows_msg):
        result = None
        for m in range(micro_count):
            if first_rows[m] <= r < first_rows[m] + window:
                hot = ones_at(iota((WIDE, WIDE), 0) + (m * WIDE + 1) == code_ref[0, r : r + 1, :])
                found = dot(grad_ref[m], hot)
                result = found if result is None else result + found
        mask = iota((HALF, WIDE), 0) == half_ref[0, r : r + 1, :]
        block = gather_columns(result, mask, HALF, EMB)
        linear = result[EMB * HALF : EMB * HALF + 1]
        block = jnp.where(iota((16, WIDE), 0) == EMB, linear, block)
        out_ref[0, :, r * WIDE : (r + 1) * WIDE] = block.astype(jnp.bfloat16)


def spread(grad_bags, codes, halves, capacity):
    batch_count, rows_msg, _ = codes.shape
    micro_count = grad_bags.shape[0]
    block = pl.BlockSpec((1, rows_msg, WIDE), lambda d: (d, 0, 0))
    return pl.pallas_call(
        partial(spread_kernel, capacity, micro_count),
        grid=(batch_count,),
        in_specs=[pl.BlockSpec(grad_bags.shape, lambda d: (0, 0, 0)), block, block],
        out_specs=pl.BlockSpec((1, 16, rows_msg * WIDE), lambda d: (d, 0, 0)),
        out_shape=jax.ShapeDtypeStruct((batch_count, 16, rows_msg * WIDE), jnp.bfloat16),
        compiler_params=pltpu.CompilerParams(vmem_limit_bytes=60 << 20),
        name="spread",
    )(grad_bags, codes, halves)


def scatter_kernel(columns, grads_ref, req_ref, out_ref, left_ref, right_ref, total_ref):
    rows_msg = req_ref.shape[1]
    tiles = right_ref.shape[0]

    @pl.when(pl.program_id(0) == 0)
    def _():
        total_ref[...] = jnp.zeros_like(total_ref)

    def build(r, carry):
        span = pl.ds(pl.multiple_of(r * WIDE, WIDE), WIDE)
        row = req_ref[0, pl.ds(r, 1), :]
        values = grads_ref[0, :, span].astype(jnp.float32)
        mask = iota((LANES, WIDE), 0) == row % LANES
        for c in range(columns):
            left_ref[c * LANES : (c + 1) * LANES, span] = jnp.where(
                mask, values[c : c + 1], 0.0
            ).astype(jnp.bfloat16)
        right_ref[:, span] = ones_at(iota((tiles, WIDE), 0) == row // LANES)
        return carry

    lax.fori_loop(0, rows_msg, build, 0)
    total_ref[...] += dot(left_ref[...], right_ref[...], NT)

    @pl.when(pl.program_id(0) == pl.num_programs(0) - 1)
    def _():
        for c in range(columns):
            out_ref[c] = total_ref[c * LANES : (c + 1) * LANES, :].T


def scatter_rows(delivered, served, columns, rows_dev):
    batch_count, rows_msg, _ = served.shape
    tiles = rows_dev // LANES
    slots = rows_msg * WIDE
    out = pl.pallas_call(
        partial(scatter_kernel, columns),
        grid=(batch_count,),
        in_specs=[
            pl.BlockSpec((1, 16, slots), lambda d: (d, 0, 0)),
            pl.BlockSpec((1, rows_msg, WIDE), lambda d: (d, 0, 0)),
        ],
        out_specs=pl.BlockSpec((columns, tiles, LANES), lambda d: (0, 0, 0)),
        out_shape=jax.ShapeDtypeStruct((columns, tiles, LANES), jnp.float32),
        scratch_shapes=[
            pltpu.VMEM((columns * LANES, slots), jnp.bfloat16),
            pltpu.VMEM((tiles, slots), jnp.bfloat16),
            pltpu.VMEM((columns * LANES, tiles), jnp.float32),
        ],
        compiler_params=pltpu.CompilerParams(vmem_limit_bytes=60 << 20),
        name="scatter",
    )(delivered, served)
    return out.reshape(columns, rows_dev)


def split_three(x):
    high = x.astype(jnp.bfloat16)
    rest = x - high.astype(jnp.float32)
    middle = rest.astype(jnp.bfloat16)
    low = (rest - middle.astype(jnp.float32)).astype(jnp.bfloat16)
    return high, middle, low


def dense_kernel(
    micro_count, tower_ref, scale_ref, pooled_ref, label_ref, weight_ref,
    cin_w_ref, cin_u_ref, w_one_ref, b_one_ref, w_two_ref, b_two_ref, w_three_ref, bias_ref,
    bags_ref, loss_ref, g_cin_w_ref, g_cin_u_ref, g_w_one_ref, g_b_one_ref, g_w_two_ref,
    g_b_two_ref, g_w_three_ref, g_bias_ref,
    embed_ref, total_ref, pairs_ref, sym_ref,
):
    f32 = jnp.float32
    width = micro_count * LANES

    def unpacked(row, count):
        pieces = []
        for m in range(micro_count):
            low = pooled_ref[m, row : row + HALF, :LANES]
            high = pooled_ref[m, row : row + HALF, LANES:]
            pieces.append(jnp.concatenate([low, high], axis=0)[:count])
        return jnp.concatenate(pieces, axis=1)

    for d in range(EMB):
        embed_ref[d * FPAD : (d + 1) * FPAD, :] = unpacked(d * HALF, FPAD)
    linear = jnp.concatenate(
        [
            pooled_ref[m, EMB * HALF : EMB * HALF + 1, :LANES]
            + pooled_ref[m, EMB * HALF : EMB * HALF + 1, LANES:]
            for m in range(micro_count)
        ],
        axis=1,
    )

    def pair_row(i, carry):
        total = jnp.zeros((FPAD, width), f32)
        for d in range(EMB):
            own = embed_ref[pl.ds(d * FPAD + i, 1), :]
            product = (embed_ref[d * FPAD : (d + 1) * FPAD, :] * own).astype(jnp.bfloat16)
            total = total + product.astype(f32)
        total_ref[pl.ds(pl.multiple_of(i * FPAD, 8), FPAD), :] = total
        return carry

    lax.fori_loop(0, FIELDS, pair_row, 0)
    thirds = split_three(total_ref[...])
    cin_w = cin_w_ref[...]
    cin_u = cin_u_ref[...].astype(f32)
    map_sum = sum(dot(cin_w, third) for third in thirds)
    cin_logits = jnp.sum(map_sum * cin_u, axis=0, keepdims=True)

    flat = embed_ref[...].astype(jnp.bfloat16)
    pre_one = dot(w_one_ref[...], flat, TN) + b_one_ref[...].astype(f32)
    hidden_one = jnp.maximum(pre_one, 0.0).astype(jnp.bfloat16)
    pre_two = dot(w_two_ref[...], hidden_one, TN) + b_two_ref[...].astype(f32)
    active_two = jnp.maximum(pre_two, 0.0)
    w_three = w_three_ref[...].astype(f32)
    deep_logits = jnp.sum(active_two * w_three, axis=0, keepdims=True)
    logits = cin_logits + deep_logits + linear + bias_ref[...].astype(f32)

    weight = weight_ref[...]
    label = label_ref[...]
    soft = jnp.maximum(logits, 0.0) + jnp.log1p(jnp.exp(-jnp.abs(logits)))
    loss_ref[...] = jnp.broadcast_to(
        jnp.sum(weight * (soft - label * logits), axis=1, keepdims=True), loss_ref.shape
    )
    grad_logits = weight * (jax.nn.sigmoid(logits) - label) / scale_ref[0]

    grad_maps = (grad_logits * cin_u).astype(jnp.bfloat16)
    grad_two = jnp.where(pre_two > 0, grad_logits * w_three, 0.0).astype(jnp.bfloat16)
    grad_hidden = dot(w_two_ref[...], grad_two)
    grad_one = jnp.where(pre_one > 0, grad_hidden, 0.0).astype(jnp.bfloat16)
    grad_flat = dot(w_one_ref[...], grad_one)

    grad_pairs = dot(cin_w, grad_maps, TN)
    for m in range(micro_count):
        pairs_ref[m, :PAIRS, :] = grad_pairs[:, m * LANES : (m + 1) * LANES]
        pairs_ref[m, PAIRS:, :] = jnp.zeros((FPAD * FPAD - PAIRS, LANES), f32)

    def mirror(j, carry):
        here = pl.ds(pl.multiple_of(j * FPAD, 8), FPAD)
        both = [
            pairs_ref[m, here, :] + pairs_ref[m, pl.ds(j, FPAD, stride=FPAD), :]
            for m in range(micro_count)
        ]
        sym_ref[here, :] = jnp.concatenate(both, axis=1)
        return carry

    lax.fori_loop(0, FIELDS, mirror, 0)
    empty = jnp.zeros((2 * HALF - FPAD, width), f32)

    for d in range(EMB):

        def add_row(j, total):
            here = pl.ds(pl.multiple_of(j * FPAD, 8), FPAD)
            return total + sym_ref[here, :] * embed_ref[pl.ds(d * FPAD + j, 1), :]

        grad_embed = lax.fori_loop(
            0, FIELDS, add_row, grad_flat[d * FPAD : (d + 1) * FPAD], unroll=3
        )
        grad_embed = jnp.concatenate([grad_embed, empty], axis=0)
        for m in range(micro_count):
            span = slice(m * LANES, (m + 1) * LANES)
            block = jnp.concatenate([grad_embed[:HALF, span], grad_embed[HALF:, span]], axis=1)
            bags_ref[m, d * HALF : (d + 1) * HALF, :] = block
    for m in range(micro_count):
        row = grad_logits[:, m * LANES : (m + 1) * LANES]
        row = jnp.concatenate([row, row], axis=1)
        bags_ref[m, EMB * HALF :, :] = jnp.broadcast_to(row, (8, WIDE))

    g_w_one_ref[...] = dot(flat, grad_one, NT)

    @pl.when(tower_ref[0] == 0)
    def _():
        g_cin_u_ref[...] = jnp.sum(map_sum * grad_logits, axis=1, keepdims=True)
        g_cin_w_ref[...] = sum(dot(grad_maps, third, NT) for third in thirds)

    @pl.when(tower_ref[0] != 0)
    def _():
        g_w_two_ref[...] = dot(hidden_one, grad_two, NT)
        g_b_one_ref[...] = jnp.sum(grad_one.astype(f32), axis=1, keepdims=True)
        g_b_two_ref[...] = jnp.sum(grad_two.astype(f32), axis=1, keepdims=True)
        g_w_three_ref[...] = jnp.sum(active_two * grad_logits, axis=1, keepdims=True)
        g_bias_ref[...] = jnp.broadcast_to(
            jnp.sum(grad_logits, axis=1, keepdims=True), g_bias_ref.shape
        )


def dense_step(tower_at, total_weight, pooled, labels, weights, params):
    micro_count = pooled.shape[0]
    width = micro_count * LANES
    cin_w, cin_u, w_one, b_one, w_two, b_two, w_three, bias = params
    in_vmem = pl.BlockSpec(memory_space=pltpu.VMEM)
    in_smem = pl.BlockSpec(memory_space=pltpu.SMEM)
    f32 = jnp.float32
    shapes = [
        ((micro_count, BAG_ROWS, WIDE), f32),
        ((1, LANES), f32),
        ((MAPS, PAIRS), f32),
        ((MAPS, 1), f32),
        ((EMB * FPAD, HID), f32),
        ((HID, 1), f32),
        ((HID, HID), f32),
        ((HID, 1), f32),
        ((HID, 1), f32),
        ((1, LANES), f32),
    ]
    return pl.pallas_call(
        partial(dense_kernel, micro_count),
        in_specs=[in_smem, in_smem] + [in_vmem] * 11,
        out_specs=[in_vmem] * len(shapes),
        out_shape=[jax.ShapeDtypeStruct(*shape) for shape in shapes],
        scratch_shapes=[
            pltpu.VMEM((EMB * FPAD, width), f32),
            pltpu.VMEM((PAIRS, width), f32),
            pltpu.VMEM((micro_count, FPAD * FPAD, LANES), f32),
            pltpu.VMEM((PAIRS, width), f32),
        ],
        compiler_params=pltpu.CompilerParams(vmem_limit_bytes=60 << 20),
        name="dense",
    )(
        tower_at.reshape(1), total_weight.reshape(1), pooled, labels, weights,
        cin_w, cin_u, w_one, b_one, w_two, b_two, w_three, bias,
    )


def unpack(flat):
    amounts = [MAPS * FIELDS * FIELDS, MAPS, FIELDS * EMB * HID, HID, HID * HID, HID, HID, 1]
    pieces = []
    offset = 0
    for amount in amounts:
        pieces.append(flat[offset : offset + amount])
        offset += amount
    cin_w = pieces[0].reshape(MAPS, FIELDS, FIELDS)
    cin_w = jnp.pad(cin_w, ((0, 0), (0, 0), (0, FPAD - FIELDS))).reshape(MAPS, PAIRS)
    w_one = jnp.swapaxes(pieces[2].reshape(FIELDS, EMB, HID), 0, 1)
    w_one = jnp.pad(w_one, ((0, 0), (0, FPAD - FIELDS), (0, 0))).reshape(EMB * FPAD, HID)
    return (
        cin_w,
        pieces[1].reshape(MAPS, 1),
        w_one,
        pieces[3].reshape(HID, 1),
        pieces[4].reshape(HID, HID),
        pieces[5].reshape(HID, 1),
        pieces[6].reshape(HID, 1),
        pieces[7].reshape(1, 1),
    )


def shards(
    shard_ids,
    local_rows,
    bag_counts,
    click_labels,
    sample_weights,
    embed_table,
    table_first,
    table_second,
    dense_params,
    dense_first,
    dense_second,
):
    tower_count = lax.axis_size("tower")
    batch_count = lax.axis_size("batch")
    tower_at = lax.axis_index("tower")
    micro_count, samples = shard_ids.shape[:2]
    columns, rows_dev = embed_table.shape
    capacity = 4 * samples * IDS_SAMP // (tower_count * batch_count)
    share = dense_params.shape[0]
    padded = -(-share // 1024) * 1024
    half_size = share * batch_count

    gathered = lax.all_gather(
        jnp.pad(dense_params.astype(jnp.bfloat16), (0, padded - share)),
        ("tower", "batch"),
        axis=0,
        tiled=True,
    )
    total_weight = lax.psum(jnp.sum(sample_weights.astype(jnp.float32)), "batch")

    id_count = samples * IDS_SAMP
    id_rows = -(-id_count // (8 * LANES)) * 8

    def arranged(values, filler):
        flat = values.reshape(micro_count, id_count)
        flat = jnp.pad(
            flat, ((0, 0), (0, id_rows * LANES - id_count)), constant_values=filler
        )
        return flat.reshape(micro_count, id_rows, LANES)

    bag_ends = jnp.cumsum(bag_counts, axis=-1)
    positions = jnp.arange(IDS_SAMP, dtype=jnp.int32)
    field_of = jnp.sum(
        (positions[None, None, :, None] >= bag_ends[:, :, None, :]).astype(jnp.int32), axis=-1
    )
    sample_of = jnp.arange(samples, dtype=jnp.int32)[None, :, None]
    is_late = (field_of >= HALF).astype(jnp.int32)
    lane_codes = arranged(sample_of + LANES * is_late, 0)
    half_fields = arranged(field_of - HALF * is_late, 0)
    targets = arranged(
        jnp.where(
            shard_ids // batch_count == tower_at, shard_ids % batch_count, batch_count
        ),
        batch_count,
    )
    requests, codes, halves = route(
        targets, arranged(local_rows, 0), lane_codes, half_fields, capacity, batch_count
    )
    requests, codes, halves = (jnp.swapaxes(x, 0, 1) for x in (requests, codes, halves))

    tiles = rows_dev // LANES
    table_tiles = jnp.swapaxes(
        embed_table.astype(jnp.bfloat16).reshape(columns, tiles, LANES), 1, 2
    ).reshape(columns * LANES, tiles)

    served = lax.all_to_all(requests, "batch", split_axis=0, concat_axis=0, tiled=True)
    answers = lax.all_to_all(
        lookup(served, table_tiles), "batch", split_axis=0, concat_axis=0, tiled=True
    )
    pooled = lax.psum(pool(answers, codes, halves, capacity, micro_count), "tower")

    def in_lanes(values):
        values = jnp.pad(values.astype(jnp.float32), ((0, 0), (0, LANES - samples)))
        return values.reshape(1, micro_count * LANES)

    flat = gathered.reshape(-1, padded)[:, :share].reshape(-1)
    (
        grad_bags, loss, g_cin_w, g_cin_u, g_w_one, g_b_one, g_w_two, g_b_two, g_w_three, g_bias,
    ) = dense_step(
        tower_at, total_weight, pooled, in_lanes(click_labels), in_lanes(sample_weights),
        unpack(flat),
    )
    sendable = spread(grad_bags.astype(jnp.bfloat16), codes, halves, capacity)
    delivered = lax.all_to_all(sendable, "batch", split_axis=0, concat_axis=0, tiled=True)
    table_grad = scatter_rows(delivered, served, columns, rows_dev)

    g_w_one = jnp.swapaxes(
        g_w_one.reshape(EMB, FPAD, HID)[:, :FIELDS], 0, 1
    ).reshape(-1)
    head = half_size - MAPS * FIELDS * FIELDS - MAPS
    rest = half_size - (FIELDS * EMB * HID - head) - HID - HID * HID - HID - HID - 1

    def pack_cin():
        flat_w = g_cin_w.reshape(MAPS, FIELDS, FPAD)[:, :, :FIELDS].reshape(-1)
        return jnp.concatenate([flat_w, g_cin_u.reshape(-1), g_w_one[:head]])

    def pack_deep():
        return jnp.concatenate(
            [
                g_w_one[head:], g_b_one.reshape(-1), g_w_two.reshape(-1), g_b_two.reshape(-1),
                g_w_three.reshape(-1), g_bias[0, :1], jnp.zeros((rest,), jnp.float32),
            ]
        )

    packed = lax.cond(tower_at == 0, pack_cin, pack_deep)
    packed = jnp.pad(packed.reshape(batch_count, share), ((0, 0), (0, padded - share)))
    own_grad = lax.psum_scatter(
        packed.reshape(-1, LANES), "batch", scatter_dimension=0, tiled=True
    ).reshape(-1)[:share]

    table_new, table_first_new, table_second_new = adam_update(
        embed_table, table_first, table_second, table_grad, rate_table
    )
    dense_new, dense_first_new, dense_second_new = adam_update(
        dense_params, dense_first, dense_second, own_grad, rate_dense
    )
    loss_sum = lax.psum(loss[0, 0], "batch") / total_weight
    return (
        table_new,
        table_first_new,
        table_second_new,
        table_new.astype(jnp.bfloat16),
        dense_new,
        dense_first_new,
        dense_second_new,
        dense_new.astype(jnp.bfloat16),
        loss_sum,
    )


def solution(mesh):
    rows = P(None, ("tower", "batch"))
    dense = P(("tower", "batch"))
    placed = (
        P(None, "batch", None, None),
        P(None, "batch", None, None),
        P(None, "batch", None),
        P(None, "batch"),
        P(None, "batch"),
        rows,
        rows,
        rows,
        dense,
        dense,
        dense,
    )
    return jax.shard_map(
        shards,
        mesh=mesh,
        in_specs=placed,
        out_specs=(rows, rows, rows, rows, dense, dense, dense, dense, P()),
        check_vma=False,
    )
```

time: 1860 us -> 523 us (0.28)
  local copies, waits for them, and re-layouts: 1290 us -> 77.9 us
  other arithmetic: 326 us -> 10 us
  Pallas kernels: 0 us -> 224 us
  matrix products: 53.2 us -> 0 us
  blocking collectives: 45 us -> 87.2 us
  starting transfers between devices: 55.2 us -> 17.4 us
    gather x21 -> x0, local copies, waits for them, and re-layouts: 1040 us -> none  [the longest x3 401 us: shards(): jnp.take_along_axis(wanted_rows, sources.reshape(micro_count, -1), axis=1)]
    scatter-add x1 -> x0, other arithmetic: 274 us -> none  [scatter_rows(): jnp.zeros((columns, rows_dev), jnp.float32).at[:, places]]
    pallas_call x0 -> x6, Pallas kernels: none -> 224 us  [the longest x1 80.8 us: lookup(): pl.pallas_call(partial(lookup_kernel, columns), grid=(batch_count,), in_s...]
    concatenate x11 -> x1, local copies, waits for them, and re-layouts: 90.3 us -> 9.5 us  [pack_cin(): return jnp.concatenate([flat_w, g_cin_u.reshape(-1), g_w_one[:head]])]
    dot_general x22 -> x0, matrix products: 48.3 us -> none  [the longest x3 16.5 us: cin_backward(): jnp.einsum('sij,sjd->sid', symmetric, embedded, precision=highest)]
    psum x1, blocking collectives: 2.58 us -> 42.8 us  [shards(): loss_sum = lax.psum(loss[0, 0], 'batch') / total_weight]
    all_to_all x9 -> x3, starting transfers between devices: 53.8 us -> 17.3 us  [the longest x1 8.3 us: shards(): lax.all_to_all(requests, 'batch', split_axis=0, concat_axis=0, tiled=True)]
    unnamed x8 -> x4, waiting for transfers between devices: 9.33 us -> 35.8 us
  transfers between devices with their start and end apart: 14 -> 6, of which waited for: 7 -> 3; matrix products, arithmetic and copies ran while one was open for 78% -> 13% of each run, Pallas kernels for 0% -> 3%
where the time goes in v1:
time: 523 us; the launch traced here: 513 us
  Pallas kernels  224 us (43%)
  blocking collectives  87.2 us (17%)
  local copies, waits for them, and re-layouts  77.9 us (15%)
  waiting for transfers between devices  77.7 us (15%)
  between operations  18.7 us (4%)
  starting transfers between devices  17.4 us (3%)
  other arithmetic  10 us (2%)
    pallas_call x1, Pallas kernels, lookup(): pl.pallas_call(partial(lookup_kernel, columns), grid=(batch_count,), in_s...  80.8 us
    pallas_call x1, Pallas kernels, scatter_rows(): pl.pallas_call(partial(scatter_kernel, columns), grid=(batch_count,), in_...  75.7 us
    psum x1, blocking collectives, shards(): lax.psum(jnp.sum(sample_weights.astype(jnp.float32)), 'batch')  44.5 us
    psum x1, blocking collectives, shards(): loss_sum = lax.psum(loss[0, 0], 'batch') / total_weight  42.8 us
    unnamed x4, waiting for transfers between devices  35.8 us
    all_to_all x1, waiting for transfers between devices, shards(): lax.all_to_all(lookup(served, table_tiles), 'batch', split_axis=0, concat...  33.5 us
    pallas_call x1, Pallas kernels, route(): pl.pallas_call(partial(route_kernel, capacity, batch_count, micro_count),...  20.3 us
    pallas_call x1, Pallas kernels, dense_step(): pl.pallas_call(partial(dense_kernel, micro_count), in_specs=[in_smem, in_...  17.2 us
  transfers between devices with their start and end apart: 6, of which 3 were waited for; matrix products, arithmetic and copies ran while one was open for 13% of the time, Pallas kernels for 3%

profile of v1, /device:TPU:0, one launch (start us, length us, event | category | flops | bytes accessed | tf_op | source)
XLA Modules:
  0.0 513.2 jit_solution(9186568395983973171)
XLA Ops:
  17.2 20.3 %route.1 = (s32[13,16,256]{2,1,0:T(8,128)}, s32[13,16,256]{2,1,0:T(8,128)}, s32[13,16,256]{2,1,0:T(8,128)}) custom-call(s32[3,72,128]{2,1,0:T(8,128)} %get-tuple-element.117.ids_ref, s32[3,72,128]{2,1,0:T(8,128)} %get-tuple-element.116.rows_ref, s32[3,72,128]{2,1,0:T(8,128)} %bitcast.87, s32[3,72,128]{2,1,0:T(8,128)} %bitcast.86), custom_call_target="tpu_custom_call" | custom-call | tf_op jit(solution)/shard_map/route/pallas_call | solution.py:146
  37.5 1.8 copy.118
  39.2 8.3 %all-to-all-start = ((s32[16,13,256]{2,1,0:T(8,128)}), s32[16,13,256]{2,1,0:T(8,128)S(1)}, u32[]{:S(2)}, u32[]{:S(2)}) async-start(s32[16,13,256]{2,1,0:T(8,128)} %bitcast.62), calls=%async_computation | async-start | bytes 524288 | tf_op jit(solution)/shard_map/all_to_all | solution.py:584
  49.1 8.4 %all-to-all-done.req_ref = s32[16,13,256]{2,1,0:T(8,128)S(1)} async-done(((s32[16,13,256]{2,1,0:T(8,128)}), s32[16,13,256]{2,1,0:T(8,128)S(1)}, u32[]{:S(2)}, u32[]{:S(2)}) %all-to-all-start) | async-done | bytes 213024 | tf_op jit(solution)/shard_map/all_to_all | solution.py:584
  58.1 80.8 %lookup.1 = bf16[16,16,3328]{2,1,0:T(8,128)(2,1)} custom-call(s32[16,13,256]{2,1,0:T(8,128)} %copy-done.2, bf16[1408,256]{1,0:T(8,128)(2,1)} %bitcast.78), custom_call_target="tpu_custom_call" | custom-call | tf_op jit(solution)/shard_map/lookup/pallas_call | solution.py:191
  139.0 4.6 all-to-all-start.1
  146.0 33.5 %all-to-all-done.1.ans_ref = bf16[16,16,3328]{2,1,0:T(8,128)(2,1)} async-done(((bf16[16,16,3328]{2,1,0:T(8,128)(2,1)}), bf16[16,16,3328]{2,1,0:T(8,128)(2,1)}, u32[]{:S(2)}, u32[]{:S(2)}) %all-to-all-start.1) | async-done | bytes 1703968 | tf_op jit(solution)/shard_map/all_to_all | solution.py:585
  179.5 14.9 %pool.1 = f32[3,248,256]{2,1,0:T(8,128)} custom-call(bf16[16,16,3328]{2,1,0:T(8,128)(2,1)} %all-to-all-done.1.ans_ref, s32[16,13,256]{2,1,0:T(8,128)} %bitcast.80, s32[16,13,256]{2,1,0:T(8,128)} %bitcast.82), custom_call_target="tpu_custom_call" | custom-call | tf_op jit(solution)/shard_map/pool/pallas_call | solution.py:231
  195.1 44.5 %psum.21 = f32[]{:T(128)} all-reduce(f32[]{:T(128)} %convert_reduce_fusion.1), channel_id=1, replica_groups=mesh['tower'=2,'batch'=16] {'batch'}, use_global_device_ids=true, to_apply=%region_1.2 | all-reduce | flops 1 | bytes 8 | tf_op jit(solution)/shard_map/psum | solution.py:547
  240.1 2.4 reshape.149
  242.5 3.0 reshape.150
  251.8 2.6 reshape.157.w_two_ref
  254.4 1.7 reshape.154
  257.2 4.2 reshape.151
  261.4 4.2 copy.95
  266.6 2.3 copy.83.cin_w_ref
  268.9 17.2 %dense.1 = (f32[3,248,256]{2,1,0:T(8,128)}, f32[1,128]{1,0:T(1,128)}, f32[200,1560]{1,0:T(8,128)}, f32[200,1]{1,0:T(8,128)S(1)}, f32[400,400]{1,0:T(8,128)}, /*i...) custom-call(s32[1]{0:T(128)} %bitcast.6.tower_ref, ...), custom_call_target="tpu_custom_call" | custom-call | tf_op jit(solution)/shard_map/dense/pallas_call | solution.py:476
  286.1 1.9 convert_element_type.45.grad_ref
  288.0 15.3 %spread.1 = bf16[16,16,3328]{2,1,0:T(8,128)(2,1)} custom-call(bf16[3,248,256]{2,1,0:T(8,128)(2,1)} %convert_element_type.45.grad_ref, s32[16,13,256]{2,1,0:T(8,128)} %bitcast.81, s32[16,13,256]{2,1,0:T(8,128)} %bitcast.83), custom_call_target="tpu_custom_call" | custom-call | tf_op jit(solution)/shard_map/spread/pallas_call | solution.py:263
  303.3 4.4 all-to-all-start.2
  307.8 1.6 copy.115
  310.9 23.9 %conditional.1 = (f32[310816]{0:T(1024)S(1)}) conditional(s32[]{:T(128)} %convert_element_type.47, (f32[156000]{0:T(1024)}, f32[400,1]{1,0:T(8,128)}, f32[400,400]{1,0:T(8,128)}, f32[400,1]{1,0:T(8,128)}, f32[400,1]{1,0:T(8,128)}, /*index=5*/f32[1,128]{1,0:T(1,128)}) %tuple.14, (f32[200,1560]{1,0:T(8,128)}, f32[200,1]{1,0:T(8,128)S(1)}, ...), branch_computations={%region_5.6_spmd, %region_6.7_spmd} | conditional | bytes 9902664 | solution.py:623
  311.7 3.0 copy.92
  314.7 5.0 copy.71
  319.6 5.7 %reshape.105 = f32[304200]{0:T(1024)} reshape(f32[200,39,39]{2,1,0:T(8,128)} %copy.71) | data formatting | bytes 2433600 | tf_op jit(solution)/shard_map/cond/branch_1_fun/reshape | solution.py:612
  325.3 9.5 %concatenate.5 = f32[310816]{0:T(1024)S(1)} concatenate(f32[304200]{0:T(1024)} %reshape.105, f32[200]{0:T(256)S(1)} %bitcast.92, f32[6416]{0:T(1024)S(1)} %slice.35), dimensions={0} | concatenate | bytes 2486528 | tf_op jit(solution)/shard_map/cond/branch_1_fun/concatenate | solution.py:613
  334.8 1.8 reshape.164
  339.2 42.8 %psum.23 = f32[]{:T(128)} all-reduce(f32[]{:T(128)S(1)} %bitcast.94), channel_id=1, replica_groups=mesh['tower'=2,'batch'=16] {'batch'}, use_global_device_ids=true, to_apply=%region_8.9 | all-reduce | flops 1 | bytes 8 | tf_op jit(solution)/shard_map/psum | solution.py:635
  383.3 35.8 %reduce-scatter.5.cloned.1.call-done = f32[152,128]{1,0:T(8,128)} async-done(((f32[2432,128]{1,0:T(8,128)}), f32[152,128]{1,0:T(8,128)}) %reduce-scatter.5.cloned.1.call-update) | async-done | bytes 77840
  419.0 1.6 fusion.6
  420.7 75.7 %scatter.1 = f32[11,256,128]{2,1,0:T(8,128)} custom-call(bf16[16,16,3328]{2,1,0:T(8,128)(2,1)} %all-to-all-done.2.grads_ref, s32[16,13,256]{2,1,0:T(8,128)} %copy-done.2), custom_call_target="tpu_custom_call" | custom-call | tf_op jit(solution)/shard_map/scatter/pallas_call | solution.py:307
  500.1 4.0 fusion.8
  (91 shorter events, 31.8 us)
Async XLA Ops:
  8.0 4.4 copy-start.9
  13.7 0.9 copy-start.10
  16.5 31.1 %copy-start = (f32[11,32768]{1,0:T(8,128)S(1)}, f32[11,32768]{1,0:T(8,128)}, u32[]{:S(2)}) copy-start(f32[11,32768]{1,0:T(8,128)} %param.18) | copy-start | bytes 4325380
  39.2 18.2 %all-to-all-start = ((s32[16,13,256]{2,1,0:T(8,128)}), s32[16,13,256]{2,1,0:T(8,128)S(1)}, u32[]{:S(2)}, u32[]{:S(2)}) async-start(s32[16,13,256]{2,1,0:T(8,128)} %bitcast.62), calls=%async_computation | async-start | bytes 524288 | tf_op jit(solution)/shard_map/all_to_all | solution.py:584
  57.4 0.7 copy-start.2
  139.0 4.6 copy-start.6
  139.0 5.4 %copy-start.8 = (s32[13,16,256]{2,1,0:T(8,128)S(1)}, s32[13,16,256]{2,1,0:T(8,128)}, u32[]{:S(2)}) copy-start(s32[13,16,256]{2,1,0:T(8,128)} %get-tuple-element.53) | copy-start | bytes 638980
  139.0 6.2 %copy-start.7 = (s32[13,16,256]{2,1,0:T(8,128)S(1)}, s32[13,16,256]{2,1,0:T(8,128)}, u32[]{:S(2)}) copy-start(s32[13,16,256]{2,1,0:T(8,128)} %get-tuple-element.54) | copy-start | bytes 638980
  139.0 40.5 %all-to-all-start.1 = ((bf16[16,16,3328]{2,1,0:T(8,128)(2,1)}), bf16[16,16,3328]{2,1,0:T(8,128)(2,1)}, u32[]{:S(2)}, u32[]{:S(2)}) async-start(bf16[16,16,3328]{2,1,0:T(8,128)(2,1)} %lookup.1), calls=%async_computation.1 | async-start | bytes 3407872 | tf_op jit(solution)/shard_map/all_to_all | solution.py:585
  143.5 96.6 %all-gather.2.cloned.1.call-start = ((), (), s32[]{:S(2)}) async-start(), calls=%async_computation.5 | async-start | bytes 1284096 | tf_op jit(solution)/shard_map/all_gather | solution.py:541
  144.3 124.6 %all-reduce.13.cloned.1.call-start = ((), (), s32[]{:S(2)}) async-start(), calls=%async_computation.4 | async-start | bytes 1523712 | tf_op jit(solution)/shard_map/psum | solution.py:588
  145.2 49.3 %copy-start.12 = (s32[3,104]{1,0:T(4,128)S(1)}, s32[3,104]{1,0:T(4,128)}, u32[]{:S(2)}) copy-start(s32[3,104]{1,0:T(4,128)} %param.17) | copy-start | bytes 3748
  145.2 94.3 %copy-start.13 = (s32[3,104]{1,0:T(4,128)S(1)}, s32[3,104]{1,0:T(4,128)}, u32[]{:S(2)}) copy-start(s32[3,104]{1,0:T(4,128)} %param.16) | copy-start | bytes 3748
  249.5 7.7 %copy-start.1 = (bf16[304200]{0:T(1024)(128)(2,1)S(1)}, bf16[304200]{0:T(1024)(128)(2,1)}, u32[]{:S(2)}) copy-start(bf16[304200]{0:T(1024)(128)(2,1)} %slice.62) | copy-start | bytes 1825204
  303.3 117.4 %all-to-all-start.2 = ((bf16[16,16,3328]{2,1,0:T(8,128)(2,1)}), bf16[16,16,3328]{2,1,0:T(8,128)(2,1)}, u32[]{:S(2)}, u32[]{:S(2)}) async-start(bf16[16,16,3328]{2,1,0:T(8,128)(2,1)} %spread.1), calls=%async_computation.2 | async-start | bytes 3407872 | tf_op jit(solution)/shard_map/all_to_all | solution.py:602
  307.7 111.3 %reduce-scatter.5.cloned.1.call-start = ((), (), s32[]{:S(2)}) async-start(), calls=%async_computation.6 | async-start | bytes 1323008
  337.9 1.3 copy-start.15
  337.9 81.1 %copy-start.11 = (f32[19426]{0:T(1024)S(1)}, f32[19426]{0:T(1024)}, u32[]{:S(2)}) copy-start(f32[19426]{0:T(1024)} %param.22) | copy-start | bytes 233116
  497.9 1.6 copy-start.3
  497.9 2.2 copy-start.4
Sparse Core Ops, SparseCore 0:
  147.8 61.1 all-gather.1
Sparse Core Ops, SparseCore 1:
  194.5 21.8 all-reduce.12
  339.3 79.7 reduce-scatter.4
